TPU v7x, 256 devices: a whole 4x4x8 slice. The times are simulated.
256 devices in a mesh: ctx: 32 (over x, z_hi, core), tp: 8 (over z_lo, y).
Axes of the slice: x: 4, y: 4, z: 8 (z_hi: 4, z_lo: 2; z = z_hi * 2 + z_lo), core: 2. Of those that a mesh axis runs over, the one named last changes fastest.
Arguments:
- tokens: bfloat16 [32768, 5120], P(('ctx', 'tp')), may hold values from -6 to 6
- queries: bfloat16 [32768, 3072], P('ctx', 'tp'), may hold values from -500 to 500
- w_key: bfloat16 [5120, 3072], P('ctx', 'tp'), may hold values from -0.078125 to 0.078125
- w_value: bfloat16 [5120, 3072], P('ctx', 'tp'), may hold values from -0.078125 to 0.078125
- tile_slot: int32 [128], replicated, may hold values from 0 to 127, as said below
- neighbour_tile: int32 [128, 6], replicated, may hold values from 0 to 127, as said below
- slab_start: int32 [128, 6], replicated, may hold values from 0 to 192
- slab_length: int32 [128, 6], replicated, may hold values from 0 to 64, as said below
- window_low: int32 [128, 6], replicated, may hold values from 0 to 127, as said below
- window_high: int32 [128, 6], replicated, may hold values from 129 to 256
Outputs:
- attended: bfloat16 [32768, 3072], P('ctx', 'tp')
Inputs may be any that keep to these rules, and one draw needn't show every extreme that they name: `tile_slot`: the slots form a permutation, and tile t has a slot in the block of 4 slots starting at (t // 4) * 4. `neighbour_tile`: call b = t // 4 the block of tile t; blocks b and b + 1 modulo 128 // 4 are adjacent. The first clip is the tiles of blocks 128 // 16 to 23, the second clip the other tiles. Each entry names a tile of the same clip whose block is the own one or adjacent to it; at most 2 entries of a tile name tiles of the previous block, and at most 2 of the next; entries naming the own block name other tiles than the own one. `slab_length`: zero leaves the entry unused. window_low is below window_high of the same entry.
All inputs are finite; a program needn't handle non-finite values.
Results may differ from a plain program's by a relative error of at most 0.0065.
The roundings to bfloat16 on the way count: a program that leaves them out, or rounds other values in their place, can miss the bound.
Values may be sent and summed in bfloat16 or wider, within the bound.
No kernel may reach another device: no remote copies, remote signals or barrier semaphores. Data moves between devices by JAX's collectives and lax.ppermute only.
A program may use at most 64 MiB of HBM per device.

v0:
```python
import math
import jax
import jax.numpy as jnp
from jax import lax
from jax.sharding import PartitionSpec as P

HD = 128
TILE = 256
NB = 6
SLAB = 64
TPD = 4


def with_halo(x, sides, width):
    for axis, dim in sides:
        peers, length = (lax.axis_size(axis), x.shape[dim])
        up = [(i, (i + 1) % peers) for i in range(peers)]
        down = [(j, i) for i, j in up]
        last = lax.slice_in_dim(x, length - width, length, axis=dim)
        initial = lax.slice_in_dim(x, 0, width, axis=dim)
        before = lax.ppermute(last, axis, up)
        after = lax.ppermute(initial, axis, down)
        x = jnp.concatenate([before, x, after], axis=dim)
    return x


def tile_entries(
    tile_slot, neighbour_tile, slab_start, slab_length, window_low, window_high, device
):
    slots_here = device * TPD + jnp.arange(TPD, dtype=jnp.int32)
    every_tile = jnp.arange(tile_slot.shape[0], dtype=jnp.int32)
    matches = tile_slot[None, :] == slots_here[:, None]
    tile_ids = jnp.sum(jnp.where(matches, every_tile[None, :], 0), axis=1)
    source_slot = jnp.take(tile_slot, jnp.take(neighbour_tile, tile_ids, axis=0), axis=0)
    return (
        source_slot,
        jnp.take(slab_start, tile_ids, axis=0),
        jnp.take(slab_length, tile_ids, axis=0),
        jnp.take(window_low, tile_ids, axis=0),
        jnp.take(window_high, tile_ids, axis=0),
    )


def per_device(
    tokens,
    queries,
    w_key,
    w_value,
    tile_slot,
    neighbour_tile,
    slab_start,
    slab_length,
    window_low,
    window_high,
):
    pair_width = w_key.shape[1]
    gathered = lax.all_gather(tokens, "tp", axis=0, tiled=True)
    key_sum = jnp.dot(
        gathered,
        lax.all_gather(w_key, "ctx", axis=0, tiled=True),
        preferred_element_type=jnp.float32,
    )
    value_sum = jnp.dot(
        gathered,
        lax.all_gather(w_value, "ctx", axis=0, tiled=True),
        preferred_element_type=jnp.float32,
    )
    key_value = jnp.concatenate(
        [key_sum.astype(jnp.bfloat16), value_sum.astype(jnp.bfloat16)], axis=1
    )
    device = lax.axis_index("ctx")
    cycle_size = lax.axis_size("ctx")
    local_rows = key_value.shape[0]
    tables = tile_entries(
        tile_slot, neighbour_tile, slab_start, slab_length, window_low, window_high, device
    )
    source_slot, starts, lengths, window_lows, window_highs = tables
    source_device = source_slot // TPD
    offsets = jnp.arange(SLAB, dtype=jnp.int32)
    source = with_halo(key_value, (("ctx", 0),), local_rows)
    relative = (source_device - device + 1 + cycle_size) % cycle_size
    first_rows = (relative * TPD + source_slot % TPD) * TILE + starts
    indices = (first_rows[:, :, None] + offsets[None, None, :]).reshape(-1)
    slab_rows = jnp.take(source, indices, axis=0, mode="clip").reshape(
        TPD, NB * SLAB, 2 * pair_width
    )
    own_tile = key_value.reshape(TPD, TILE, 2 * pair_width)
    candidates = jnp.concatenate([own_tile, slab_rows], axis=1)
    head_count = pair_width // HD
    all_keys = candidates[:, :, :pair_width].reshape(TPD, -1, head_count, HD)
    all_values = candidates[:, :, pair_width:].reshape(TPD, -1, head_count, HD)
    query_tiles = queries.reshape(TPD, TILE, head_count, HD)
    scores = jnp.einsum(
        "prhd,pshd->phrs", query_tiles, all_keys, preferred_element_type=jnp.float32
    ) * (1.0 / math.sqrt(HD))
    query_row = jnp.arange(TILE, dtype=jnp.int32)[None, :, None]
    in_window = (query_row >= window_lows[:, None, :]) & (query_row < window_highs[:, None, :])
    valid_slab = offsets[None, None, :] < lengths[:, :, None]
    allowed_slab = (in_window[:, :, :, None] & valid_slab[:, None, :, :]).reshape(
        TPD, TILE, NB * SLAB
    )
    allowed = jnp.concatenate([jnp.ones((TPD, TILE, TILE), dtype=bool), allowed_slab], axis=2)
    scores = jnp.where(allowed[:, None, :, :], scores, -jnp.inf)
    row_top = jnp.max(scores, axis=-1, keepdims=True)
    weights = jnp.exp(scores - row_top)
    row_total = jnp.sum(weights, axis=-1, keepdims=True)
    probability = weights.astype(jnp.bfloat16)
    weighted = jnp.einsum(
        "phrs,pshd->prhd", probability, all_values, preferred_element_type=jnp.float32
    )
    result = weighted / jnp.transpose(row_total, (0, 2, 1, 3))
    return result.reshape(TPD * TILE, pair_width).astype(jnp.bfloat16)


def solution(mesh):
    in_specs = (
        P(("ctx", "tp"), None),
        P("ctx", "tp"),
        P("ctx", "tp"),
        P("ctx", "tp"),
        P(),
        P(),
        P(),
        P(),
        P(),
        P(),
    )
    out_specs = P("ctx", "tp")
    return jax.shard_map(
        per_device, mesh=mesh, in_specs=in_specs, out_specs=out_specs, check_vma=False
    )
```

profile of v0, /device:TPU:32, one launch (start us, length us, event | category | flops | bytes accessed | tf_op | source)
XLA Modules:
  0.0 345.4 jit_solution(11280214016702032859)
XLA Ops:
  6.5 0.7 all-gather.8.cloned.1.call-update
  7.3 0.0 all-gather.4.cloned.1.call-start
  7.3 0.7 all-gather.4.cloned.1.call-update
  8.0 0.0 all-gather.6.cloned.1.call-start
  8.1 0.7 all-gather.6.cloned.1.call-update
  8.8 0.8 select_reduce_fusion
  9.6 61.7 %all-gather.8.cloned.1.call-done = bf16[5120,384]{1,0:T(8,128)(2,1)} async-done(((bf16[160,384]{1,0:T(8,128)(2,1)}), bf16[5120,384]{1,0:T(8,128)(2,1)}) %all-gather.8.cloned.1.call-update) | async-done | bytes 3932176 | tf_op jit(solution)/shard_map/all_gather | solution.py:65
  71.3 113.4 %all-gather.4.cloned.1.call-done = bf16[1024,5120]{1,0:T(8,128)(2,1)} async-done(((bf16[128,5120]{1,0:T(8,128)(2,1)}), bf16[1024,5120]{1,0:T(8,128)(2,1)}) %all-gather.4.cloned.1.call-update) | async-done | bytes 10485776 | tf_op jit(solution)/shard_map/all_gather | solution.py:57
  184.8 9.4 %convolution_convert_fusion = bf16[1024,384]{0,1:T(8,128)(2,1)S(1)} fusion(bf16[1024,5120]{1,0:T(8,128)(2,1)} %all-gather.4.cloned.1.call-done, bf16[5120,384]{1,0:T(8,128)(2,1)} %all-gather.8.cloned.1.call-done), kind=kOutput, calls=%fused_computation.27 | convolution fusion | flops 4026925056 | bytes 15204352 | tf_op jit(solution)/shard_map/dot_general | solution.py:63
  194.1 0.0 copy-start.2
  194.1 0.0 copy-start.6
  194.1 0.0 copy-start.7
  194.2 0.0 copy-start.8
  194.2 51.8 %all-gather.6.cloned.1.call-done = bf16[5120,384]{1,0:T(8,128)(2,1)} async-done(((bf16[160,384]{1,0:T(8,128)(2,1)}), bf16[5120,384]{1,0:T(8,128)(2,1)}) %all-gather.6.cloned.1.call-update) | async-done | bytes 3932176 | tf_op jit(solution)/shard_map/all_gather | solution.py:60
  246.0 9.3 %convolution_convert_fusion.1 = bf16[1024,384]{0,1:T(8,128)(2,1)S(1)} fusion(bf16[1024,5120]{1,0:T(8,128)(2,1)} %all-gather.4.cloned.1.call-done, bf16[5120,384]{1,0:T(8,128)(2,1)} %all-gather.6.cloned.1.call-done), kind=kOutput, calls=%fused_computation.28 | convolution fusion | flops 4026925056 | bytes 15204352 | tf_op jit(solution)/shard_map/dot_general | solution.py:58
  255.3 0.0 copy-done.2
  255.3 0.0 copy-start.4
  255.3 0.0 copy-start
  255.4 0.0 copy-start.9
  255.4 0.0 copy-start.10
  255.4 0.0 copy-start.5
  255.4 0.1 pad_maximum_fusion.2
  255.5 0.8 copy-done.4
  256.3 3.9 %collective-permute-start.1 = (bf16[1024,768]{0,1:T(8,128)(2,1)S(1)}, bf16[1024,768]{0,1:T(8,128)(2,1)}, u32[]{:S(2)}, u32[]{:S(2)}) collective-permute-start(bf16[1024,768]{0,1:T(8,128)(2,1)S(1)} %pad_maximum_fusion.2), channel_id=1, source_target_pairs={{8,0},{16,8},{24,16},{32,24},{40,32},{48,40},{56,48},{64,56},{72,6... | collective-permute-start | bytes 4718600 | tf_op jit(solution)/shard_map/ppermute | solution.py:22
  260.2 0.0 collective-permute-start
  260.2 0.0 copy-done.6
  260.2 0.1 copy.40
  260.4 0.1 copy.36
  260.5 0.6 gather_fusion.4
  261.0 0.6 gather_fusion.3
  261.6 0.1 copy.35
  261.7 0.6 gather_fusion.2
  262.3 0.1 compare_select_fusion
  262.4 0.1 reshape.124
  262.5 0.7 gather_fusion
  263.2 0.1 reshape.123
  263.2 0.1 copy.41
  263.4 0.6 gather_fusion.5
  263.9 0.1 copy.42
  264.0 0.6 gather_fusion.6
  264.6 0.1 broadcast_select_fusion.1
  264.7 0.1 iota_add_fusion
  264.8 0.1 reshape.132
  264.9 0.1 lt.54
  264.9 0.1 lt.55
  265.0 0.1 add.85
  265.1 1.2 reshape.156
  266.3 0.1 fusion.15
  266.4 0.3 bitcast_and_fusion
  266.7 0.2 concatenate.15
  266.9 1.2 copy.63
  268.1 26.5 %collective-permute-done.1 = bf16[1024,768]{0,1:T(8,128)(2,1)} collective-permute-done((bf16[1024,768]{0,1:T(8,128)(2,1)S(1)}, bf16[1024,768]{0,1:T(8,128)(2,1)}, u32[]{:S(2)}, u32[]{:S(2)}) %collective-permute-start.1) | collective-permute-done | bytes 1572896 | tf_op jit(solution)/shard_map/ppermute | solution.py:22
  294.7 6.2 %collective-permute-done = bf16[1024,768]{0,1:T(8,128)(2,1)} collective-permute-done((bf16[1024,768]{0,1:T(8,128)(2,1)S(1)}, bf16[1024,768]{0,1:T(8,128)(2,1)}, u32[]{:S(2)}, u32[]{:S(2)}) %collective-permute-start) | collective-permute-done | bytes 1572896 | tf_op jit(solution)/shard_map/ppermute | solution.py:21
  300.9 9.7 %pad_maximum_fusion = bf16[3072,768]{0,1:T(8,128)(2,1)} fusion(bf16[1024,768]{0,1:T(8,128)(2,1)} %collective-permute-done.1, bf16[1024,384]{0,1:T(8,128)(2,1)S(1)} %copy-done.3, bf16[1024,384]{0,1:T(8,128)(2,1)} %copy-done.4, bf16[1024,768]{0,1:T(8,128)(2,1)} %collective-permute-done), kind=kLoop, calls=%fused_computation.12 | loop fusion | flops 18874368 | bytes 9437184 | tf_op jit(solution)/shard_map/concatenate | solution.py:23
  310.6 6.7 %copy.37 = bf16[3072,768]{1,0:T(8,128)(2,1)} copy(bf16[3072,768]{0,1:T(8,128)(2,1)} %pad_maximum_fusion) | data formatting | bytes 9437184 | tf_op jit(solution)/shard_map/concatenate | solution.py:23
  317.3 9.0 %gather_fusion.1 = bf16[1536,768]{1,0:T(8,128)(2,1)S(1)} fusion(bf16[3072,768]{1,0:T(8,128)(2,1)} %copy.37, s32[2048]{0:T(1024)S(1)} %pad_clamp_fusion), kind=kCustom, calls=%fused_computation.6 | custom fusion | bytes 4724736 | tf_op jit(solution)/shard_map/jit(_take)/gather | solution.py:84
  326.3 2.5 copy.39
  328.8 2.3 pad_maximum_fusion.1
  331.2 0.1 copy-done.1
  331.2 1.8 fusion.2
  333.1 1.8 fusion
  334.8 2.4 fusion.10
  337.2 0.7 copy.53
  337.9 1.0 copy.64
  (18 shorter events, 0.1 us)
Async XLA Ops:
  6.5 64.8 %all-gather.8.cloned.1.call-start = ((), (), s32[]{:S(2)}) async-start(), calls=%async_computation.2 | async-start | bytes 4055040 | tf_op jit(solution)/shard_map/all_gather | solution.py:65
  7.3 177.5 %all-gather.4.cloned.1.call-start = ((), (), s32[]{:S(2)}) async-start(), calls=%async_computation | async-start | bytes 11796480 | tf_op jit(solution)/shard_map/all_gather | solution.py:57
  8.0 238.0 %all-gather.6.cloned.1.call-start = ((), (), s32[]{:S(2)}) async-start(), calls=%async_computation.1 | async-start | bytes 4055040 | tf_op jit(solution)/shard_map/all_gather | solution.py:60
  194.1 61.2 %copy-start.2 = (bf16[1024,384]{0,1:T(8,128)(2,1)}, bf16[1024,384]{0,1:T(8,128)(2,1)S(1)}, u32[]{:S(2)}) copy-start(bf16[1024,384]{0,1:T(8,128)(2,1)S(1)} %convolution_convert_fusion) | copy-start | bytes 2359300
  194.1 66.1 %copy-start.6 = (s32[128,6]{0,1:T(8,128)S(1)}, s32[128,6]{0,1:T(8,128)}, u32[]{:S(2)}) copy-start(s32[128,6]{0,1:T(8,128)} %param.20) | copy-start | bytes 9220
  194.1 66.2 %copy-start.7 = (s32[128,6]{0,1:T(8,128)S(1)}, s32[128,6]{0,1:T(8,128)}, u32[]{:S(2)}) copy-start(s32[128,6]{0,1:T(8,128)} %param.18) | copy-start | bytes 9220
  194.2 67.4 %copy-start.8 = (s32[128,6]{0,1:T(8,128)S(1)}, s32[128,6]{0,1:T(8,128)}, u32[]{:S(2)}) copy-start(s32[128,6]{0,1:T(8,128)} %param.17) | copy-start | bytes 9220
  255.3 0.9 copy-start.4
  255.3 7.1 %copy-start = (s32[128]{0:T(128)S(1)}, s32[128]{0:T(128)}, u32[]{:S(2)}) copy-start(s32[128]{0:T(128)} %param.16) | copy-start | bytes 1540
  255.4 7.9 %copy-start.9 = (s32[128,6]{0,1:T(8,128)S(1)}, s32[128,6]{0,1:T(8,128)}, u32[]{:S(2)}) copy-start(s32[128,6]{0,1:T(8,128)} %param.21) | copy-start | bytes 9220
  255.4 8.6 %copy-start.10 = (s32[128,6]{0,1:T(8,128)S(1)}, s32[128,6]{0,1:T(8,128)}, u32[]{:S(2)}) copy-start(s32[128,6]{0,1:T(8,128)} %param.19) | copy-start | bytes 9220
  255.4 9.7 %copy-start.5 = (bf16[1024,384]{1,0:T(8,128)(2,1)S(1)}, bf16[1024,384]{1,0:T(8,128)(2,1)}, u32[]{:S(2)}) copy-start(bf16[1024,384]{1,0:T(8,128)(2,1)} %param.13) | copy-start | bytes 2359300
  256.3 38.4 %collective-permute-start.1 = (bf16[1024,768]{0,1:T(8,128)(2,1)S(1)}, bf16[1024,768]{0,1:T(8,128)(2,1)}, u32[]{:S(2)}, u32[]{:S(2)}) collective-permute-start(bf16[1024,768]{0,1:T(8,128)(2,1)S(1)} %pad_maximum_fusion.2), channel_id=1, source_target_pairs={{8,0},{16,8},{24,16},{32,24},{40,32},{48,40},{56,48},{64,56},{72,6... | collective-permute-start | bytes 4718600 | tf_op jit(solution)/shard_map/ppermute | solution.py:22
  260.2 40.7 %collective-permute-start = (bf16[1024,768]{0,1:T(8,128)(2,1)S(1)}, bf16[1024,768]{0,1:T(8,128)(2,1)}, u32[]{:S(2)}, u32[]{:S(2)}) collective-permute-start(bf16[1024,768]{0,1:T(8,128)(2,1)S(1)} %pad_maximum_fusion.2), channel_id=1, source_target_pairs={{0,8},{8,16},{16,24},{24,32},{32,40},{40,48},{48,56},{56,64},{64,7... | collective-permute-start | bytes 4718600 | tf_op jit(solution)/shard_map/ppermute | solution.py:21
  263.2 37.7 %copy-start.3 = (bf16[1024,384]{0,1:T(8,128)(2,1)S(1)}, bf16[1024,384]{0,1:T(8,128)(2,1)}, u32[]{:S(2)}) copy-start(bf16[1024,384]{0,1:T(8,128)(2,1)} %copy-done.2) | copy-start | bytes 2359300
  328.8 2.4 copy-start.1
Sparse Core Ops, SparseCore 0:
  9.9 61.4 all-gather.7
  73.1 111.5 all-gather.3
  187.3 58.6 all-gather.5
where the time goes:
time: 346 us; the launch traced here: 345 us
  waiting for transfers between devices  262 us (76%)
  local copies, waits for them, and re-layouts  28 us (8%)
  matrix products  22.9 us (7%)
  other arithmetic  15.4 us (4%)
  between operations  13.3 us (4%)
  starting transfers between devices  4.01 us (1%)
    all_gather x1, waiting for transfers between devices, per_device(): gathered = lax.all_gather(tokens, 'tp', axis=0, tiled=True)  113 us
    all_gather x1, waiting for transfers between devices, per_device(): lax.all_gather(w_value, 'ctx', axis=0, tiled=True)  61.7 us
    all_gather x1, waiting for transfers between devices, per_device(): lax.all_gather(w_key, 'ctx', axis=0, tiled=True)  51.8 us
    ppermute x1, waiting for transfers between devices, with_halo(): after = lax.ppermute(initial, axis, down)  26.5 us
    concatenate x1, other arithmetic, with_halo(): x = jnp.concatenate([before, x, after], axis=dim)  9.67 us
    dot_general x1, matrix products, per_device(): jnp.dot(gathered, lax.all_gather(w_value, 'ctx', axis=0, tiled=True), pre...  9.35 us
    dot_general x1, matrix products, per_device(): jnp.dot(gathered, lax.all_gather(w_key, 'ctx', axis=0, tiled=True), prefe...  9.35 us
    gather x1, local copies, waits for them, and re-layouts, per_device(): jnp.take(source, indices, axis=0, mode='clip')  9.03 us
  transfers between devices with their start and end apart: 5, of which 5 were waited for; matrix products, arithmetic and copies ran while one was open for 5% of the time, Pallas kernels for 0%

commit v1 on v0

--- a/solution.py
+++ b/solution.py
@@ -54,7 +54,9 @@
     window_high,
 ):
     pair_width = w_key.shape[1]
-    gathered = lax.all_gather(tokens, "tp", axis=0, tiled=True)
+    gathered = jnp.concatenate(
+        lax.all_to_all(jnp.stack([tokens] * lax.axis_size("tp")), "tp", 0, 0), axis=0
+    )
     key_sum = jnp.dot(
         gathered,
         lax.all_gather(w_key, "ctx", axis=0, tiled=True),

time: 346 us -> 282 us (0.82)
  waiting for transfers between devices: 262 us -> 185 us
  starting transfers between devices: 4.01 us -> 13.9 us
  local copies, waits for them, and re-layouts: 28 us -> 34.4 us
  other arithmetic: 15.4 us -> 11.6 us
    all_gather x1 -> x0, waiting for transfers between devices: 113 us -> none  [per_device(): gathered = lax.all_gather(tokens, 'tp', axis=0, tiled=True)]
    all_to_all x0 -> x1, waiting for transfers between devices: none -> 81.7 us  [per_device(): lax.all_to_all(jnp.stack([tokens] * lax.axis_size('tp')), 'tp', 0, 0)]
    all_gather x1, waiting for transfers between devices: 51.8 us -> 0.02 us  [per_device(): lax.all_gather(w_key, 'ctx', axis=0, tiled=True)]
    all_to_all x0 -> x1, starting transfers between devices: none -> 7 us  [per_device(): lax.all_to_all(jnp.stack([tokens] * lax.axis_size('tp')), 'tp', 0, 0)]
    another operation x0 -> x1, local copies, waits for them, and re-layouts: none -> 6.57 us  [per_device(): jnp.stack([tokens] * lax.axis_size('tp'))]
    all_gather x1, waiting for transfers between devices: 61.7 us -> 68.3 us  [per_device(): lax.all_gather(w_value, 'ctx', axis=0, tiled=True)]
  transfers between devices with their start and end apart: 5 -> 5, of which waited for: 5 -> 4; matrix products, arithmetic and copies ran while one was open for 5% -> 6% of each run, Pallas kernels for 0% -> 0%
where the time goes in v1:
time: 282 us
  waiting for transfers between devices  185 us (66%)
  local copies, waits for them, and re-layouts  34.4 us (12%)
  matrix products  23.3 us (8%)
  starting transfers between devices  13.9 us (5%)
  between operations  13.6 us (5%)
  other arithmetic  11.6 us (4%)
    all_to_all x1, waiting for transfers between devices, per_device(): lax.all_to_all(jnp.stack([tokens] * lax.axis_size('tp')), 'tp', 0, 0)  81.7 us
    all_gather x1, waiting for transfers between devices, per_device(): lax.all_gather(w_value, 'ctx', axis=0, tiled=True)  68.3 us
    ppermute x1, waiting for transfers between devices, with_halo(): after = lax.ppermute(initial, axis, down)  26.9 us
    dot_general x1, matrix products, per_device(): jnp.dot(gathered, lax.all_gather(w_key, 'ctx', axis=0, tiled=True), prefe...  9.62 us
    dot_general x1, matrix products, per_device(): jnp.dot(gathered, lax.all_gather(w_value, 'ctx', axis=0, tiled=True), pre...  9.46 us
    gather x1, local copies, waits for them, and re-layouts, per_device(): jnp.take(source, indices, axis=0, mode='clip')  9.03 us
    all_to_all x1, starting transfers between devices, per_device(): lax.all_to_all(jnp.stack([tokens] * lax.axis_size('tp')), 'tp', 0, 0)  7 us
    ppermute x1, starting transfers between devices, with_halo(): after = lax.ppermute(initial, axis, down)  6.9 us
  transfers between devices with their start and end apart: 5, of which 4 were waited for; matrix products, arithmetic and copies ran while one was open for 6% of the time, Pallas kernels for 0%

profile of v1, /device:TPU:32, one launch (start us, length us, event | category | flops | bytes accessed | tf_op | source)
XLA Modules:
  0.0 281.6 jit_solution(1688202834785503432)
XLA Ops:
  6.5 6.6 %stack.2 = bf16[8,128,5120]{2,1,0:T(8,128)(2,1)} broadcast(bf16[128,5120]{1,0:T(8,128)(2,1)} %param.12), dimensions={1,2} | broadcast | bytes 11796480 | tf_op jit(solution)/shard_map/stack | solution.py:58
  13.1 7.0 %all-to-all-start = ((bf16[8,128,5120]{2,1,0:T(8,128)(2,1)}), bf16[8,128,5120]{2,1,0:T(8,128)(2,1)}, u32[]{:S(2)}, u32[]{:S(2)}) async-start(bf16[8,128,5120]{2,1,0:T(8,128)(2,1)} %stack.2), calls=%async_computation | async-start | bytes 20971520 | tf_op jit(solution)/shard_map/all_to_all | solution.py:58
  20.1 0.0 all-gather.5.cloned.1.call-start
  20.1 0.7 all-gather.5.cloned.1.call-update
  20.8 0.0 all-gather.3.cloned.1.call-start
  20.9 0.7 all-gather.3.cloned.1.call-update
  21.6 0.0 copy-done
  21.6 0.2 select_reduce_fusion
  21.8 68.3 %all-gather.5.cloned.1.call-done = bf16[5120,384]{1,0:T(8,128)(2,1)} async-done(((bf16[160,384]{1,0:T(8,128)(2,1)}), bf16[5120,384]{1,0:T(8,128)(2,1)}) %all-gather.5.cloned.1.call-update) | async-done | bytes 3932176 | tf_op jit(solution)/shard_map/all_gather | solution.py:67
  90.1 81.7 %all-to-all-done = bf16[8,128,5120]{2,1,0:T(8,128)(2,1)} async-done(((bf16[8,128,5120]{2,1,0:T(8,128)(2,1)}), bf16[8,128,5120]{2,1,0:T(8,128)(2,1)}, u32[]{:S(2)}, u32[]{:S(2)}) %all-to-all-start) | async-done | bytes 10485792 | tf_op jit(solution)/shard_map/all_to_all | solution.py:58
  171.8 9.5 %convolution_convert_fusion = bf16[1024,384]{0,1:T(8,128)(2,1)S(1)} fusion(bf16[1024,5120]{1,0:T(8,128)(2,1)} %bitcast, bf16[5120,384]{1,0:T(8,128)(2,1)} %all-gather.5.cloned.1.call-done), kind=kOutput, calls=%fused_computation.27 | convolution fusion | flops 4026925056 | bytes 15204352 | tf_op jit(solution)/shard_map/dot_general | solution.py:65
  181.3 0.0 copy-start.2
  181.3 0.0 copy-start.5
  181.3 0.0 copy-start.6
  181.3 0.0 copy-start.7
  181.3 0.0 all-gather.3.cloned.1.call-done
  181.4 9.6 %convolution_convert_fusion.1 = bf16[1024,384]{0,1:T(8,128)(2,1)S(1)} fusion(bf16[1024,5120]{1,0:T(8,128)(2,1)} %bitcast, bf16[5120,384]{1,0:T(8,128)(2,1)} %all-gather.3.cloned.1.call-done), kind=kOutput, calls=%fused_computation.28 | convolution fusion | flops 4026925056 | bytes 15204352 | tf_op jit(solution)/shard_map/dot_general | solution.py:60
  191.0 0.0 copy-start.8
  191.0 0.0 copy-start.9
  191.0 0.0 copy-start.4
  191.1 0.1 pad_maximum_fusion.2
  191.2 0.8 copy-done.3
  192.0 6.9 %collective-permute-start.1 = (bf16[1024,768]{0,1:T(8,128)(2,1)S(1)}, bf16[1024,768]{0,1:T(8,128)(2,1)}, u32[]{:S(2)}, u32[]{:S(2)}) collective-permute-start(bf16[1024,768]{0,1:T(8,128)(2,1)S(1)} %pad_maximum_fusion.2), channel_id=1, source_target_pairs={{8,0},{16,8},{24,16},{32,24},{40,32},{48,40},{56,48},{64,56},{72,6... | collective-permute-start | bytes 4718600 | tf_op jit(solution)/shard_map/ppermute | solution.py:22
  198.9 0.0 collective-permute-start
  198.9 0.0 copy-done.5
  198.9 0.1 copy.40
  199.0 0.0 copy-done.6
  199.0 0.1 copy.36
  199.1 0.6 gather_fusion.4
  199.7 0.6 gather_fusion.3
  200.3 0.1 copy.35
  200.4 0.6 gather_fusion.2
  200.9 0.1 compare_select_fusion
  201.0 0.1 reshape.130
  201.1 0.7 gather_fusion
  201.8 0.1 reshape.129
  201.9 0.1 copy.41
  202.0 0.6 gather_fusion.5
  202.6 0.1 copy.42
  202.7 0.6 gather_fusion.6
  203.3 0.1 broadcast_select_fusion.1
  203.4 0.1 iota_add_fusion
  203.4 0.1 reshape.138
  203.5 0.1 lt.54
  203.6 0.1 lt.55
  203.7 0.1 add.85
  203.7 1.1 reshape.162
  204.8 0.1 fusion.15
  204.9 0.3 bitcast_and_fusion
  205.2 0.2 concatenate.15
  205.4 1.2 copy.63
  206.7 26.9 %collective-permute-done.1 = bf16[1024,768]{0,1:T(8,128)(2,1)} collective-permute-done((bf16[1024,768]{0,1:T(8,128)(2,1)S(1)}, bf16[1024,768]{0,1:T(8,128)(2,1)}, u32[]{:S(2)}, u32[]{:S(2)}) %collective-permute-start.1) | collective-permute-done | bytes 1572896 | tf_op jit(solution)/shard_map/ppermute | solution.py:22
  233.6 6.3 %collective-permute-done = bf16[1024,768]{0,1:T(8,128)(2,1)} collective-permute-done((bf16[1024,768]{0,1:T(8,128)(2,1)S(1)}, bf16[1024,768]{0,1:T(8,128)(2,1)}, u32[]{:S(2)}, u32[]{:S(2)}) %collective-permute-start) | collective-permute-done | bytes 1572896 | tf_op jit(solution)/shard_map/ppermute | solution.py:21
  239.9 6.5 %pad_maximum_fusion = bf16[3072,768]{0,1:T(8,128)(2,1)} fusion(bf16[1024,768]{0,1:T(8,128)(2,1)} %collective-permute-done.1, bf16[1024,384]{0,1:T(8,128)(2,1)} %copy-done.2, bf16[1024,384]{0,1:T(8,128)(2,1)} %copy-done.3, bf16[1024,768]{0,1:T(8,128)(2,1)} %collective-permute-done), kind=kLoop, calls=%fused_computation.12 | loop fusion | flops 18874368 | bytes 9437184 | tf_op jit(solution)/shard_map/concatenate | solution.py:23
  246.4 6.7 %copy.37 = bf16[3072,768]{1,0:T(8,128)(2,1)} copy(bf16[3072,768]{0,1:T(8,128)(2,1)} %pad_maximum_fusion) | data formatting | bytes 9437184 | tf_op jit(solution)/shard_map/concatenate | solution.py:23
  253.2 9.0 %gather_fusion.1 = bf16[1536,768]{1,0:T(8,128)(2,1)S(1)} fusion(bf16[3072,768]{1,0:T(8,128)(2,1)} %copy.37, s32[2048]{0:T(1024)S(1)} %pad_clamp_fusion), kind=kCustom, calls=%fused_computation.6 | custom fusion | bytes 4724736 | tf_op jit(solution)/shard_map/jit(_take)/gather | solution.py:86
  262.2 2.5 copy.39
  264.7 2.3 pad_maximum_fusion.1
  267.0 0.1 copy-done.1
  267.1 1.8 fusion.2
  268.9 1.8 fusion
  270.7 2.4 fusion.10
  273.1 0.7 copy.53
  273.8 1.0 copy.64
  (16 shorter events, 0.1 us)
Async XLA Ops:
  13.1 8.5 %copy-start = (s32[128]{0:T(128)S(1)}, s32[128]{0:T(128)}, u32[]{:S(2)}) copy-start(s32[128]{0:T(128)} %param.16) | copy-start | bytes 1540
  13.1 158.7 %all-to-all-start = ((bf16[8,128,5120]{2,1,0:T(8,128)(2,1)}), bf16[8,128,5120]{2,1,0:T(8,128)(2,1)}, u32[]{:S(2)}, u32[]{:S(2)}) async-start(bf16[8,128,5120]{2,1,0:T(8,128)(2,1)} %stack.2), calls=%async_computation | async-start | bytes 20971520 | tf_op jit(solution)/shard_map/all_to_all | solution.py:58
  20.1 70.0 %all-gather.5.cloned.1.call-start = ((), (), s32[]{:S(2)}) async-start(), calls=%async_computation.2 | async-start | bytes 4055040 | tf_op jit(solution)/shard_map/all_gather | solution.py:67
  20.8 160.5 %all-gather.3.cloned.1.call-start = ((), (), s32[]{:S(2)}) async-start(), calls=%async_computation.1 | async-start | bytes 4055040 | tf_op jit(solution)/shard_map/all_gather | solution.py:62
  181.3 9.7 %copy-start.2 = (bf16[1024,384]{0,1:T(8,128)(2,1)}, bf16[1024,384]{0,1:T(8,128)(2,1)S(1)}, u32[]{:S(2)}) copy-start(bf16[1024,384]{0,1:T(8,128)(2,1)S(1)} %convolution_convert_fusion) | copy-start | bytes 2359300
  181.3 17.6 %copy-start.5 = (s32[128,6]{0,1:T(8,128)S(1)}, s32[128,6]{0,1:T(8,128)}, u32[]{:S(2)}) copy-start(s32[128,6]{0,1:T(8,128)} %param.20) | copy-start | bytes 9220
  181.3 17.7 %copy-start.6 = (s32[128,6]{0,1:T(8,128)S(1)}, s32[128,6]{0,1:T(8,128)}, u32[]{:S(2)}) copy-start(s32[128,6]{0,1:T(8,128)} %param.18) | copy-start | bytes 9220
  181.3 18.9 %copy-start.7 = (s32[128,6]{0,1:T(8,128)S(1)}, s32[128,6]{0,1:T(8,128)}, u32[]{:S(2)}) copy-start(s32[128,6]{0,1:T(8,128)} %param.17) | copy-start | bytes 9220
  191.0 1.0 copy-start.3
  191.0 10.9 %copy-start.8 = (s32[128,6]{0,1:T(8,128)S(1)}, s32[128,6]{0,1:T(8,128)}, u32[]{:S(2)}) copy-start(s32[128,6]{0,1:T(8,128)} %param.21) | copy-start | bytes 9220
  191.0 11.5 %copy-start.9 = (s32[128,6]{0,1:T(8,128)S(1)}, s32[128,6]{0,1:T(8,128)}, u32[]{:S(2)}) copy-start(s32[128,6]{0,1:T(8,128)} %param.19) | copy-start | bytes 9220
  191.0 12.7 %copy-start.4 = (bf16[1024,384]{1,0:T(8,128)(2,1)S(1)}, bf16[1024,384]{1,0:T(8,128)(2,1)}, u32[]{:S(2)}) copy-start(bf16[1024,384]{1,0:T(8,128)(2,1)} %param.13) | copy-start | bytes 2359300
  192.0 41.6 %collective-permute-start.1 = (bf16[1024,768]{0,1:T(8,128)(2,1)S(1)}, bf16[1024,768]{0,1:T(8,128)(2,1)}, u32[]{:S(2)}, u32[]{:S(2)}) collective-permute-start(bf16[1024,768]{0,1:T(8,128)(2,1)S(1)} %pad_maximum_fusion.2), channel_id=1, source_target_pairs={{8,0},{16,8},{24,16},{32,24},{40,32},{48,40},{56,48},{64,56},{72,6... | collective-permute-start | bytes 4718600 | tf_op jit(solution)/shard_map/ppermute | solution.py:22
  198.9 41.0 %collective-permute-start = (bf16[1024,768]{0,1:T(8,128)(2,1)S(1)}, bf16[1024,768]{0,1:T(8,128)(2,1)}, u32[]{:S(2)}, u32[]{:S(2)}) collective-permute-start(bf16[1024,768]{0,1:T(8,128)(2,1)S(1)} %pad_maximum_fusion.2), channel_id=1, source_target_pairs={{0,8},{8,16},{16,24},{24,32},{32,40},{40,48},{48,56},{56,64},{64,7... | collective-permute-start | bytes 4718600 | tf_op jit(solution)/shard_map/ppermute | solution.py:21
  264.7 2.4 copy-start.1
Sparse Core Ops, SparseCore 0:
  23.4 66.6 all-gather.4
  92.6 64.7 all-gather.2
